TPU v7x, 32 devices: a whole 2x2x4 slice. The times are simulated.
32 devices in a mesh: harm: 8 (over y, x, core), mode: 4 (over z).
Axes of the slice: x: 2, y: 2, z: 4, core: 2. Of those that a mesh axis runs over, the one named last changes fastest.
Arguments:
- mode_vectors: float32 [49152, 1024], P('harm', 'mode'), may hold values from -0.09375 to 0.09375
- weights: float32 [49152, 1024], P('harm', 'mode'), may hold values from -0.1875 to 0.1875
- cotangent: float32 [49152, 1024], P('harm', 'mode'), may hold values from -6 to 6
- eigenvalues: float32 [1024], replicated, may hold values from 0 to 4
- eigen_cotangent: float32 [1024], replicated, may hold values from -6 to 6
- slab_rows: int32 [4096], replicated, may hold values from 0 to 49151, as said below
Outputs:
- slab: float32 [4096, 49152], P('mode', 'harm')
Inputs may be any that keep to these rules, and one draw needn't show every extreme that they name: `slab_rows`: each block of 6144 consecutive harmonics (0 to 6143, 6144 to 12287 and so on) holds exactly 512 of the slab rows.
All inputs are finite; a program needn't handle non-finite values.
Results may differ from a plain program's by a relative error of at most 0.0001.
Values sent between devices are 32-bit elements; how exact they have to be, the bound alone decides.
A program may use at most 128 MiB of HBM per device.

v0:
```python
import jax
import jax.numpy as jnp
from jax import lax
from jax.sharding import PartitionSpec as P

regular = 0.01
precision = lax.Precision.HIGHEST


def product(left, right, left_dim, right_dim):
    return lax.dot_general(
        left,
        right,
        (((left_dim,), (right_dim,)), ((), ())),
        precision=precision,
        preferred_element_type=jnp.float32,
    )


def weigh_gap(block, row_ids, col_ids, eigenvalues, eigen_cotangent):
    eigen_rows = lax.dynamic_slice_in_dim(eigenvalues, row_ids, block.shape[0])
    eigen_cols = lax.dynamic_slice_in_dim(eigenvalues, col_ids, block.shape[1])
    slope_cols = lax.dynamic_slice_in_dim(eigen_cotangent, col_ids, block.shape[1])
    differ = eigen_cols[None, :] - eigen_rows[:, None]
    factor = differ / (differ * differ + regular)
    rows = row_ids + lax.broadcasted_iota(jnp.int32, block.shape, 0)
    cols = col_ids + lax.broadcasted_iota(jnp.int32, block.shape, 1)
    return factor * block + jnp.where(rows == cols, slope_cols[None, :], 0.0)


def pick_rows(table, slab_rows, harm_index):
    row_count = table.shape[0]
    offset = slab_rows - harm_index * row_count
    inside = (offset >= 0) & (offset < row_count)
    picked = jnp.take(table, jnp.clip(offset, 0, row_count - 1), axis=0)
    return jnp.where(inside[:, None], picked, 0.0)


def gather_weights(weights, slab_rows, harm_index, harm_count, mode_count):
    width = weights.shape[1]
    with jax.named_scope("pick"):
        picked = pick_rows(weights, slab_rows, harm_index)
    piece = slab_rows.shape[0] // (harm_count * mode_count)
    picked = picked.reshape(mode_count, harm_count, piece, width)
    with jax.named_scope("sum_weights"):
        picked = lax.psum_scatter(picked, "harm", scatter_dimension=1, tiled=True)
    picked = picked.reshape(mode_count, piece, width)
    with jax.named_scope("swap"):
        swapped = lax.all_to_all(picked, "mode", split_axis=0, concat_axis=2, tiled=True)
    with jax.named_scope("spread_weights"):
        return lax.all_gather(
            swapped.reshape(piece, mode_count * width), "harm", axis=0, tiled=True
        )


def plain(
    mode_vectors,
    weights,
    cotangent,
    eigenvalues,
    eigen_cotangent,
    slab_rows,
    harm_count,
    mode_count,
):
    harm_index = lax.axis_index("harm")
    width = mode_vectors.shape[1]
    modes = width * mode_count
    full = lax.all_gather(mode_vectors, "mode", axis=1, tiled=True)
    owned_weights = gather_weights(weights, slab_rows, harm_index, harm_count, mode_count)
    gram = product(full, cotangent, 0, 0)
    gram = lax.psum_scatter(gram, "harm", scatter_dimension=0, tiled=True)
    weighted = weigh_gap(
        gram,
        harm_index * (modes // harm_count),
        lax.axis_index("mode") * width,
        eigenvalues,
        eigen_cotangent,
    )
    weighted = lax.all_gather(weighted, "mode", axis=1, tiled=True)
    weighted = lax.all_gather(weighted, "harm", axis=0, tiled=True)
    return product(product(owned_weights, weighted, 1, 0), full, 1, 1)


def solution(mesh):
    harm_count = mesh.shape["harm"]
    mode_count = mesh.shape["mode"]
    placed = (P("harm", "mode"), P("harm", "mode"), P("harm", "mode"), P(), P(), P())

    def local(*operands):
        return plain(*operands, harm_count, mode_count)

    return jax.shard_map(
        local, mesh=mesh, in_specs=placed, out_specs=P("mode", "harm"), check_vma=False
    )
```

profile of v0, /device:TPU:0, one launch (start us, length us, event | category | flops | bytes accessed | tf_op | source)
XLA Modules:
  0.0 702.6 jit_solution(5876162007898497041)
XLA Ops:
  7.4 0.7 all-gather.6.cloned.1.call-update
  8.1 0.0 reduce-scatter.3.cloned.1.call-start
  8.2 18.9 %gather_fusion = f32[4096,256]{1,0:T(8,128)} fusion(f32[6144,256]{1,0:T(8,128)} %param.7, s32[4096]{0:T(1024)S(1)} %fusion.3), kind=kCustom, calls=%fused_computation | custom fusion | bytes 8404992 | tf_op jit(solution)/shard_map/pick/jit(_take)/gather | solution.py:35
  27.2 5.6 copy.10
  32.7 5.5 select_select_fusion
  38.3 0.0 reduce-scatter.5.cloned.1.call-start
  38.3 399.3 %all-gather.6.cloned.1.call-done = f32[6144,1024]{1,0:T(8,128)} async-done(((f32[6144,256]{1,0:T(8,128)}), f32[6144,1024]{1,0:T(8,128)}) %all-gather.6.cloned.1.call-update) | async-done | bytes 25165840 | tf_op jit(solution)/shard_map/all_gather | solution.py:69
  437.7 44.0 %fusion.4 = f32[1024,256]{1,0:T(8,128)} fusion(f32[6144,1024]{1,0:T(8,128)} %all-gather.6.cloned.1.call-done, f32[6144,256]{1,0:T(8,128)} %param.8), kind=kOutput, calls=%fused_computation.13 | convolution fusion | flops 19327352832 | bytes 32505856 | tf_op jit(solution)/shard_map/dot_general | solution.py:11
  481.6 0.0 all-gather.4.cloned.1.call-start
  481.7 0.0 reduce-scatter.3.cloned.1.call-done
  481.7 19.2 %all_to_all.15 = f32[4,128,256]{1,2,0:T(8,128)} all-to-all(f32[4,128,256]{1,2,0:T(8,128)} %bitcast.19), channel_id=1, replica_groups=mesh['harm'=8,'mode'=4] {'mode'}, dimensions={0} | all-to-all | bytes 1048576 | tf_op jit(solution)/shard_map/swap/all_to_all | solution.py:49
  500.9 0.0 all-gather.4.cloned.1.call-update
  500.9 0.0 all-gather.8.cloned.1.call-start
  501.0 0.8 dynamic_slice.10
  501.7 0.8 dynamic_slice.9
  502.5 0.8 dynamic_slice.11
  503.2 12.6 %reduce-scatter.5.cloned.1.call-done = f32[128,256]{1,0:T(8,128)} async-done(((f32[1024,256]{1,0:T(8,128)}), f32[128,256]{1,0:T(8,128)}) %reduce-scatter.5.cloned.1.call-update) | async-done | bytes 131088 | tf_op jit(solution)/shard_map/reduce_scatter | solution.py:72
  515.8 1.0 fusion.2
  516.9 15.9 %all_gather.14 = f32[128,1024]{1,0:T(8,128)} all-gather(f32[128,256]{1,0:T(8,128)S(1)} %fusion.2), channel_id=1, replica_groups=mesh['harm'=8,'mode'=4] {'mode'}, dimensions={1}, use_global_device_ids=true | all-gather | bytes 655360 | tf_op jit(solution)/shard_map/all_gather | solution.py:80
  532.8 0.0 all-gather.8.cloned.1.call-update
  532.8 22.0 %all-gather.4.cloned.1.call-done = f32[1024,1024]{0,1:T(8,128)} async-done(((f32[128,1024]{0,1:T(8,128)}), f32[1024,1024]{0,1:T(8,128)}) %all-gather.4.cloned.1.call-update) | async-done | bytes 4194320 | tf_op jit(solution)/shard_map/spread_weights/all_gather | solution.py:51
  554.8 38.4 %all-gather.8.cloned.1.call-done = f32[1024,1024]{1,0:T(8,128)} async-done(((f32[128,1024]{1,0:T(8,128)}), f32[1024,1024]{1,0:T(8,128)}) %all-gather.8.cloned.1.call-update) | async-done | bytes 4194320 | tf_op jit(solution)/shard_map/all_gather | solution.py:81
  593.2 16.6 %fusion.5 = f32[1024,1024]{1,0:T(8,128)S(1)} fusion(f32[1024,1024]{0,1:T(8,128)} %all-gather.4.cloned.1.call-done, f32[1024,1024]{1,0:T(8,128)} %all-gather.8.cloned.1.call-done), kind=kOutput, calls=%fused_computation.14 | convolution fusion | flops 12884901888 | bytes 12582912 | tf_op jit(solution)/shard_map/dot_general | solution.py:11
  609.8 85.2 %fusion.6 = f32[1024,6144]{1,0:T(8,128)} fusion(f32[1024,1024]{1,0:T(8,128)S(1)} %fusion.5, f32[6144,1024]{1,0:T(8,128)} %all-gather.6.cloned.1.call-done), kind=kOutput, calls=%fused_computation.15 | convolution fusion | flops 77309411328 | bytes 54525952 | tf_op jit(solution)/shard_map/dot_general | solution.py:11
  (11 shorter events, 0.1 us)
Async XLA Ops:
  7.4 0.8 copy-start
  7.4 430.3 %all-gather.6.cloned.1.call-start = ((), (), s32[]{:S(2)}) async-start(), calls=%async_computation.5 | async-start | bytes 31457280 | tf_op jit(solution)/shard_map/all_gather | solution.py:69
  8.1 473.6 %reduce-scatter.3.cloned.1.call-start = ((), (), s32[]{:S(2)}) async-start(), calls=%async_computation.3 | async-start | bytes 4718592 | tf_op jit(solution)/shard_map/sum_weights/reduce_scatter | solution.py:46
  38.3 477.6 %reduce-scatter.5.cloned.1.call-start = ((), (), s32[]{:S(2)}) async-start(), calls=%async_computation.6 | async-start | bytes 1179648 | tf_op jit(solution)/shard_map/reduce_scatter | solution.py:72
  481.6 73.2 %all-gather.4.cloned.1.call-start = ((), (), s32[]{:S(2)}) async-start(), calls=%async_computation.4 | async-start | bytes 4718592 | tf_op jit(solution)/shard_map/spread_weights/all_gather | solution.py:51
  500.9 92.3 %all-gather.8.cloned.1.call-start = ((), (), s32[]{:S(2)}) async-start(), calls=%async_computation.7 | async-start | bytes 4718592 | tf_op jit(solution)/shard_map/all_gather | solution.py:81
Sparse Core Ops, SparseCore 0:
  9.7 427.8 all-gather.5
Sparse Core Ops, SparseCore 1:
  38.4 53.7 reduce-scatter.2
  481.7 34.1 reduce-scatter.4
  517.6 37.2 all-gather.3
  556.8 36.4 all-gather.7
where the time goes:
time: 703 us
  waiting for transfers between devices  473 us (67%)
  matrix products  146 us (21%)
  blocking collectives  35.1 us (5%)
  local copies, waits for them, and re-layouts  26.8 us (4%)
  between operations  15.1 us (2%)
    all_gather x1, waiting for transfers between devices, plain(): full = lax.all_gather(mode_vectors, 'mode', axis=1, tiled=True)  399 us
    dot_general x3, matrix products, product(): lax.dot_general(left, right, (((left_dim,), (right_dim,)), ((), ())), pre...  146 us
    all_gather x1, waiting for transfers between devices, plain(): weighted = lax.all_gather(weighted, 'harm', axis=0, tiled=True)  38.4 us
    gather x2, local copies, waits for them, and re-layouts, pick_rows(): picked = jnp.take(table, jnp.clip(offset, 0, row_count - 1), axis=0)  24.5 us
    all_gather x1, waiting for transfers between devices, gather_weights(): lax.all_gather(swapped.reshape(piece, mode_count * width), 'harm', axis=0...  22 us
    all_to_all x1, blocking collectives, gather_weights(): lax.all_to_all(picked, 'mode', split_axis=0, concat_axis=2, tiled=True)  19.2 us
    all_gather x1, blocking collectives, plain(): weighted = lax.all_gather(weighted, 'mode', axis=1, tiled=True)  15.9 us
  transfers between devices with their start and end apart: 5, of which 4 were waited for; matrix products, arithmetic and copies ran while one was open for 11% of the time, Pallas kernels for 0%

commit v1 on v0

--- a/solution.py
+++ b/solution.py
@@ -46,7 +46,12 @@
         picked = lax.psum_scatter(picked, "harm", scatter_dimension=1, tiled=True)
     picked = picked.reshape(mode_count, piece, width)
     with jax.named_scope("swap"):
-        swapped = lax.all_to_all(picked, "mode", split_axis=0, concat_axis=2, tiled=True)
+        swapped = jnp.concatenate(
+            lax.all_to_all(
+                jnp.stack(jnp.split(picked, lax.axis_size("mode"), axis=0)), "mode", 0, 0
+            ),
+            axis=2,
+        )
     with jax.named_scope("spread_weights"):
         return lax.all_gather(
             swapped.reshape(piece, mode_count * width), "harm", axis=0, tiled=True

time: 703 us -> 703 us (level)
  no operation moved by 1% of the time
where the time goes in v1:
time: 703 us
  waiting for transfers between devices  472 us (67%)
  matrix products  146 us (21%)
  blocking collectives  34.2 us (5%)
  local copies, waits for them, and re-layouts  29.1 us (4%)
  between operations  15.1 us (2%)
    all_gather x1, waiting for transfers between devices, plain(): full = lax.all_gather(mode_vectors, 'mode', axis=1, tiled=True)  399 us
    dot_general x3, matrix products, product(): lax.dot_general(left, right, (((left_dim,), (right_dim,)), ((), ())), pre...  146 us
    all_gather x1, waiting for transfers between devices, plain(): weighted = lax.all_gather(weighted, 'harm', axis=0, tiled=True)  38.4 us
    gather x2, local copies, waits for them, and re-layouts, pick_rows(): picked = jnp.take(table, jnp.clip(offset, 0, row_count - 1), axis=0)  24.5 us
    all_gather x1, waiting for transfers between devices, gather_weights(): lax.all_gather(swapped.reshape(piece, mode_count * width), 'harm', axis=0...  22 us
    all_to_all x1, blocking collectives, gather_weights(): lax.all_to_all(jnp.stack(jnp.split(picked, lax.axis_size('mode'), axis=0)...  18.2 us
    all_gather x1, blocking collectives, plain(): weighted = lax.all_gather(weighted, 'mode', axis=1, tiled=True)  16 us
  transfers between devices with their start and end apart: 5, of which 4 were waited for; matrix products, arithmetic and copies ran while one was open for 11% of the time, Pallas kernels for 0%

profile of v1, /device:TPU:0, one launch (start us, length us, event | category | flops | bytes accessed | tf_op | source)
XLA Modules:
  0.0 702.7 jit_solution(4570062755073579900)
XLA Ops:
  7.4 0.7 all-gather.6.cloned.1.call-update
  8.1 0.0 all-reduce.3.cloned.1.call-start
  8.2 18.9 %gather_fusion = f32[4096,256]{1,0:T(8,128)} fusion(f32[6144,256]{1,0:T(8,128)} %param.7, s32[4096]{0:T(1024)S(1)} %fusion.3), kind=kCustom, calls=%fused_computation | custom fusion | bytes 8404992 | tf_op jit(solution)/shard_map/pick/jit(_take)/gather | solution.py:35
  27.1 5.6 copy.13
  32.7 5.5 select_select_fusion
  38.2 0.0 reduce-scatter.5.cloned.1.call-start
  38.3 399.4 %all-gather.6.cloned.1.call-done = f32[6144,1024]{1,0:T(8,128)} async-done(((f32[6144,256]{1,0:T(8,128)}), f32[6144,1024]{1,0:T(8,128)}) %all-gather.6.cloned.1.call-update) | async-done | bytes 25165840 | tf_op jit(solution)/shard_map/all_gather | solution.py:74
  437.7 44.0 %fusion.4 = f32[1024,256]{1,0:T(8,128)} fusion(f32[6144,1024]{1,0:T(8,128)} %all-gather.6.cloned.1.call-done, f32[6144,256]{1,0:T(8,128)} %param.8), kind=kOutput, calls=%fused_computation.14 | convolution fusion | flops 19327352832 | bytes 32505856 | tf_op jit(solution)/shard_map/dot_general | solution.py:11
  481.7 0.0 all-gather.4.cloned.1.call-start
  481.7 0.6 dynamic-slice
  482.3 1.7 constant_dynamic-slice_fusion
  484.1 18.2 %all_to_all.5 = f32[4,1,128,256]{2,3,1,0:T(8,128)} all-to-all(f32[4,1,128,256]{2,3,1,0:T(8,128)S(1)} %constant_dynamic-slice_fusion), channel_id=1, replica_groups=mesh['harm'=8,'mode'=4] {'mode'}, dimensions={0} | all-to-all | bytes 1048576 | tf_op jit(solution)/shard_map/swap/all_to_all | solution.py:50
  502.3 0.0 all-gather.4.cloned.1.call-update
  502.3 0.0 all-gather.8.cloned.1.call-start
  502.3 0.8 dynamic_slice.10
  503.1 0.8 dynamic_slice.9
  503.9 0.8 dynamic_slice.11
  504.6 11.2 %reduce-scatter.5.cloned.1.call-done = f32[128,256]{1,0:T(8,128)} async-done(((f32[1024,256]{1,0:T(8,128)}), f32[128,256]{1,0:T(8,128)}) %reduce-scatter.5.cloned.1.call-update) | async-done | bytes 131088 | tf_op jit(solution)/shard_map/reduce_scatter | solution.py:77
  515.9 1.0 fusion.2
  516.9 16.0 %all_gather.14 = f32[128,1024]{1,0:T(8,128)} all-gather(f32[128,256]{1,0:T(8,128)S(1)} %fusion.2), channel_id=1, replica_groups=mesh['harm'=8,'mode'=4] {'mode'}, dimensions={1}, use_global_device_ids=true | all-gather | bytes 655360 | tf_op jit(solution)/shard_map/all_gather | solution.py:85
  532.9 22.0 %all-gather.4.cloned.1.call-done = f32[1024,1024]{0,1:T(8,128)} async-done(((f32[128,1024]{0,1:T(8,128)}), f32[1024,1024]{0,1:T(8,128)}) %all-gather.4.cloned.1.call-update) | async-done | bytes 4194320 | tf_op jit(solution)/shard_map/spread_weights/all_gather | solution.py:56
  554.8 38.4 %all-gather.8.cloned.1.call-done = f32[1024,1024]{1,0:T(8,128)} async-done(((f32[128,1024]{1,0:T(8,128)}), f32[1024,1024]{1,0:T(8,128)}) %all-gather.8.cloned.1.call-update) | async-done | bytes 4194320 | tf_op jit(solution)/shard_map/all_gather | solution.py:86
  593.3 16.6 %fusion.5 = f32[1024,1024]{1,0:T(8,128)S(1)} fusion(f32[1024,1024]{0,1:T(8,128)} %all-gather.4.cloned.1.call-done, f32[1024,1024]{1,0:T(8,128)} %all-gather.8.cloned.1.call-done), kind=kOutput, calls=%fused_computation.15 | convolution fusion | flops 12884901888 | bytes 12582912 | tf_op jit(solution)/shard_map/dot_general | solution.py:11
  609.8 85.2 %fusion.6 = f32[1024,6144]{1,0:T(8,128)} fusion(f32[1024,1024]{1,0:T(8,128)S(1)} %fusion.5, f32[6144,1024]{1,0:T(8,128)} %all-gather.6.cloned.1.call-done), kind=kOutput, calls=%fused_computation.16 | convolution fusion | flops 77309411328 | bytes 54525952 | tf_op jit(solution)/shard_map/dot_general | solution.py:11
  (13 shorter events, 0.1 us)
Async XLA Ops:
  7.4 0.8 copy-start
  7.4 430.3 %all-gather.6.cloned.1.call-start = ((), (), s32[]{:S(2)}) async-start(), calls=%async_computation.3 | async-start | bytes 31457280 | tf_op jit(solution)/shard_map/all_gather | solution.py:74
  8.1 474.2 %all-reduce.3.cloned.1.call-start = ((), (), s32[]{:S(2)}) async-start(), calls=%async_computation.6 | async-start | bytes 8388608
  38.2 443.5 %copy-start.1 = (u32[32]{0:T(128)S(1)}, u32[32]{0:T(128)}, u32[]{:S(2)}) copy-start(u32[32]{0:T(128)} %constant.42) | copy-start | bytes 388
  38.2 477.6 %reduce-scatter.5.cloned.1.call-start = ((), (), s32[]{:S(2)}) async-start(), calls=%async_computation.4 | async-start | bytes 1179648 | tf_op jit(solution)/shard_map/reduce_scatter | solution.py:77
  481.7 73.2 %all-gather.4.cloned.1.call-start = ((), (), s32[]{:S(2)}) async-start(), calls=%async_computation.2 | async-start | bytes 4718592 | tf_op jit(solution)/shard_map/spread_weights/all_gather | solution.py:56
  502.3 91.0 %all-gather.8.cloned.1.call-start = ((), (), s32[]{:S(2)}) async-start(), calls=%async_computation.5 | async-start | bytes 4718592 | tf_op jit(solution)/shard_map/all_gather | solution.py:86
Sparse Core Ops, SparseCore 0:
  9.7 427.8 all-gather.5
Sparse Core Ops, SparseCore 1:
  38.3 83.1 all-reduce.2
  481.7 34.1 reduce-scatter.4
  517.6 37.2 all-gather.3
  556.8 36.4 all-gather.7
